TPU v7x, 32 devices: a whole 2x2x4 slice. The times are simulated.
32 devices in a mesh: group: 2 (over x), seq: 4 (over y, core), fsdp: 4 (over z).
Axes of the slice: x: 2, y: 2, z: 4, core: 2. Of those that a mesh axis runs over, the one named last changes fastest.
Arguments:
- latents: bfloat16 [8192, 3072], P(('group', 'seq', 'fsdp')), parts along dimension 0, may hold values from -6 to 6
- qkv_weight: bfloat16 [3072, 3, 3072], P('seq', None, 'fsdp'), may hold values from -0.109375 to 0.109375
- out_weight: bfloat16 [3072, 3072], P('fsdp', 'seq'), may hold values from -0.109375 to 0.109375
- mod_weight: bfloat16 [256, 3, 3072], P(None, None, ('seq', 'fsdp')), may hold values from -1 to 1
- q_gain: float32 [128], replicated, may hold values from 0.5 to 12, as said below
- k_gain: float32 [128], replicated, may hold values from 0.5 to 12, as said below
- tile_slot: int32 [8, 16], P('group'), parts along dimension 0, may hold values from 0 to 15, each once within a row
- win_start: int32 [8, 16, 3], P('group'), parts along dimension 0, may hold values from 0 to 2, as said below
- step_index: int32 [2], P('group'), parts along dimension 0, may hold values from 0 to 999
Outputs:
- updated: bfloat16 [8192, 3072], P(('group', 'seq', 'fsdp')), parts along dimension 0
There are 2 independent parts, one for each index of `group`. A program takes and returns all parts, laid end to end along the dimension named above; an argument that names none is the same for every part. Nothing has to cross between parts.
Inputs may be any that keep to these rules, and one draw needn't show every extreme that they name: win_start[t, p] holds the first time slice, tile row and tile column of the window of the tile at spatial position p (row p // 4, column p % 4) of slice t; the window spans 2 slices, 3 rows and 3 columns inside the clip and contains the tile itself. `tile_slot`: each row is an ordering of the 16 spatial tiles. `q_gain`: positive gains. `k_gain`: positive gains.
All inputs are finite; a program needn't handle non-finite values.
Results may differ from a plain program's by a relative error of at most 0.014.
The roundings to bfloat16 on the way count: a program that leaves them out, or rounds other values in their place, can miss the bound.
Values may be sent and summed in bfloat16 or wider, within the bound.
A program may use at most 192 MiB of HBM per device.

v0:
```python
import math
import jax
import jax.numpy as jnp
from jax import lax
from jax.sharding import PartitionSpec as P

HD = 128
FREQ = 256
TILE = 64
GW = 4


def with_halo(block, sides, width):
    for axis, dim in sides:
        count = lax.axis_size(axis)
        forward = [(i, i + 1) for i in range(count - 1)]
        backward = [(target, source) for source, target in forward]
        low = lax.ppermute(
            lax.slice_in_dim(block, block.shape[dim] - width, None, axis=dim), axis, forward
        )
        high = lax.ppermute(lax.slice_in_dim(block, 0, width, axis=dim), axis, backward)
        block = jnp.concatenate([low, block, high], axis=dim)
    return block


def time_signal(step_index):
    halfway = FREQ // 2
    freqs_all = jnp.exp(-math.log(10000.0) * jnp.arange(halfway, dtype=jnp.float32) / halfway)
    angles = step_index[0].astype(jnp.float32) * freqs_all
    return jax.nn.silu(jnp.concatenate([jnp.cos(angles), jnp.sin(angles)])).astype(jnp.bfloat16)


def modulate(tokens_in, shift_mod, scale_mod):
    values = tokens_in.astype(jnp.float32)
    centre = jnp.mean(values, axis=-1, keepdims=True)
    spread = jnp.mean((values - centre) ** 2, axis=-1, keepdims=True)
    normal = (values - centre) * lax.rsqrt(spread + 1e-06)
    return (normal * (1.0 + scale_mod) + shift_mod).astype(jnp.bfloat16)


def rms_scale(values, gain_vec):
    return values * lax.rsqrt(jnp.mean(values * values, axis=-1, keepdims=True) + 1e-06) * gain_vec


def project_rows(normed, weight_flat, q_gain, k_gain):
    mixture = jnp.dot(normed, weight_flat, preferred_element_type=jnp.float32)
    row_count = normed.shape[0]
    mixture = mixture.reshape(row_count, 3, -1, HD)
    queries = rms_scale(mixture[:, 0], q_gain)
    key_vecs = rms_scale(mixture[:, 1], k_gain)
    return (
        jnp.stack([queries, key_vecs, mixture[:, 2]], axis=1)
        .reshape(row_count, -1)
        .astype(jnp.bfloat16)
    )


def slot_masks(tile_slot, win_start, block_idx):
    blocks_total = tile_slot.shape[0]
    spot_count = tile_slot.shape[1]
    ids_query = lax.dynamic_index_in_dim(tile_slot, block_idx, 0, keepdims=False)
    window_row = lax.dynamic_index_in_dim(win_start, block_idx, 0, keepdims=False)
    onehot = ids_query[:, None] == jnp.arange(spot_count, dtype=jnp.int32)[None, :]
    corner = jnp.sum(jnp.where(onehot[:, :, None], window_row[None], 0), axis=1)
    result = []
    for offset in (-1, 0, 1):
        key_time = block_idx + offset
        ids_key = lax.dynamic_index_in_dim(
            tile_slot, jnp.clip(key_time, 0, blocks_total - 1), 0, keepdims=False
        )
        tile_row = ids_key // GW
        tile_col = ids_key % GW
        inside = (corner[:, 0:1] <= key_time) & (key_time <= corner[:, 0:1] + 1)
        inside = (
            inside & (corner[:, 1:2] <= tile_row[None]) & (tile_row[None] <= corner[:, 1:2] + 2)
        )
        inside = (
            inside & (corner[:, 2:3] <= tile_col[None]) & (tile_col[None] <= corner[:, 2:3] + 2)
        )
        result.append(jnp.repeat(jnp.repeat(inside, TILE, axis=0), TILE, axis=1))
    return result


def body(
    latents, qkv_weight, out_weight, mod_weight, q_gain, k_gain, tile_slot, win_start, step_index
):
    signal = time_signal(step_index)
    local_cols = mod_weight.shape[2]
    own_mod = jnp.dot(
        signal[None], mod_weight.reshape(FREQ, 3 * local_cols), preferred_element_type=jnp.float32
    ).reshape(3, local_cols)
    modulation = lax.all_gather(own_mod, ("seq", "fsdp"), axis=1, tiled=True)
    shift_mod = modulation[0]
    scale_mod = modulation[1]
    gate_mod = modulation[2]
    qkv_full = lax.all_gather(qkv_weight, "seq", axis=0, tiled=True)
    out_full = lax.all_gather(out_weight, "seq", axis=1, tiled=True)
    model_width = qkv_full.shape[0]
    group_width = qkv_full.shape[2]
    head_count = group_width // HD
    weight_flat = qkv_full.reshape(model_width, 3 * group_width)
    packed = project_rows(
        modulate(lax.all_gather(latents, "fsdp", axis=0, tiled=True), shift_mod, scale_mod),
        weight_flat,
        q_gain,
        k_gain,
    )
    block_tokens = packed.shape[0]
    query_all = packed[:, :group_width].reshape(block_tokens, head_count, HD)
    kv_local = packed[:, group_width:]
    extended = with_halo(kv_local[None], (("seq", 0),), 1)
    key_all = extended[:, :, :group_width].reshape(3, block_tokens, head_count, HD)
    value_all = extended[:, :, group_width:].reshape(3, block_tokens, head_count, HD)
    visible = slot_masks(tile_slot, win_start, lax.axis_index("seq"))
    inv_root = 1.0 / math.sqrt(HD)
    query_span = 512
    head_outputs = []
    for head_idx in range(head_count):
        row_parts = []
        for query_blk in range(block_tokens // query_span):
            lower = query_blk * query_span
            queries = query_all[lower : lower + query_span, head_idx]
            running_top = jnp.full((query_span,), -1e30, jnp.float32)
            running_total = jnp.zeros((query_span,), jnp.float32)
            accum = jnp.zeros((query_span, HD), jnp.float32)
            for key_blk in range(3):
                scores = (
                    lax.dot_general(
                        queries,
                        key_all[key_blk, :, head_idx],
                        (((1,), (1,)), ((), ())),
                        preferred_element_type=jnp.float32,
                    )
                    * inv_root
                )
                allowed = visible[key_blk][lower : lower + query_span]
                shifted = jnp.where(allowed, scores, -1e30)
                new_top = jnp.maximum(running_top, jnp.max(shifted, axis=1))
                weights = jnp.where(allowed, jnp.exp(shifted - new_top[:, None]), 0.0)
                factor = jnp.exp(running_top - new_top)
                running_total = running_total * factor + jnp.sum(weights, axis=1)
                accum = accum * factor[:, None] + jnp.dot(
                    weights.astype(jnp.bfloat16),
                    value_all[key_blk, :, head_idx],
                    preferred_element_type=jnp.float32,
                )
                running_top = new_top
            row_parts.append(accum / running_total[:, None])
        head_outputs.append(jnp.concatenate(row_parts, axis=0))
    attended = (
        jnp.stack(head_outputs, axis=1).reshape(block_tokens, group_width).astype(jnp.bfloat16)
    )
    projected = lax.psum_scatter(
        jnp.dot(attended, out_full, preferred_element_type=jnp.float32).astype(jnp.bfloat16),
        "fsdp",
        scatter_dimension=0,
        tiled=True,
    ).astype(jnp.float32)
    return (latents.astype(jnp.float32) + gate_mod * projected).astype(jnp.bfloat16)


def solution(mesh):
    in_specs = (
        P(("group", "seq", "fsdp"), None),
        P("seq", None, "fsdp"),
        P("fsdp", "seq"),
        P(None, None, ("seq", "fsdp")),
        P(),
        P(),
        P("group", None),
        P("group", None, None),
        P("group"),
    )
    out_specs = P(("group", "seq", "fsdp"), None)
    return jax.shard_map(body, mesh=mesh, in_specs=in_specs, out_specs=out_specs, check_vma=False)
```

profile of v0, /device:TPU:0, one launch (start us, length us, event | category | flops | bytes accessed | tf_op | source)
XLA Modules:
  0.0 624.4 jit_solution(11329790541286253678)
XLA Ops:
  7.3 6.1 copy.163
  14.4 37.1 %all-gather = f32[16,192,3]{1,2,0:T(4,128)S(1)} all-gather(f32[1,192,3]{1,2,0:T(4,128)S(1)} %bitcast.464), channel_id=1, replica_groups=mesh['group'=2,'seq'=4,'fsdp'=4] {'seq','fsdp'}, dimensions={0}, use_global_device_ids=true | all-gather | bytes 39168 | tf_op jit(solution)/shard_map/all_gather | solution.py:92
  52.3 75.7 %all-gather.5.cloned.1.call-done = bf16[1024,3072]{1,0:T(8,128)(2,1)} async-done(((bf16[256,3072]{1,0:T(8,128)(2,1)}), bf16[1024,3072]{1,0:T(8,128)(2,1)}) %all-gather.5.cloned.1.call-update) | async-done | bytes 6291472 | tf_op jit(solution)/shard_map/all_gather | solution.py:103
  127.9 3.8 convert_reduce_fusion
  134.3 84.6 %all-gather.7.cloned.1.call-done = bf16[3072,3,768]{0,2,1:T(8,128)(2,1)} async-done(((bf16[768,3,768]{0,2,1:T(8,128)(2,1)}), bf16[3072,3,768]{0,2,1:T(8,128)(2,1)}) %all-gather.7.cloned.1.call-update) | async-done | bytes 14155792 | tf_op jit(solution)/shard_map/all_gather | solution.py:96
  218.9 20.0 %fusion.7 = f32[1024,3,6,128]{0,3,2,1:T(8,128)S(1)} fusion(bf16[3,6,128,3072]{3,2,1,0:T(8,128)(2,1)} %bitcast.468, bf16[1024,3072]{1,0:T(8,128)(2,1)} %all-gather.5.cloned.1.call-done, f32[3072]{0:T(1024)S(1)} %bitcast.465, f32[3072]{0:T(1024)S(1)} %bitcast.466, f32[1024]{0:T(1024)S(1)} %add_rsqrt_fusion.2, f32[1024]{0:T(1024)S(1)} %broadcast_multiply_fusion), kind=kOutput, calls=%fused_computation.10 | convolution fusion | flops 14514388992 | bytes 29917184 | tf_op jit(solution)/shard_map/dot_general | solution.py:46
  244.4 3.9 collective-permute-start
  249.6 12.3 %reduce-scatter.2.cloned.1.call-start = ((), (), s32[]{:S(2)}) async-start(), calls=%async_computation.4 | async-start | bytes 7864320 | tf_op jit(solution)/shard_map/reduce_scatter | solution.py:153
  275.4 7.7 %pad_maximum_fusion = bf16[3,1024,1536]{1,2,0:T(8,128)(2,1)} fusion(bf16[1,1024,1536]{1,2,0:T(8,128)(2,1)} %collective-permute-done.1, bf16[1,1024,1536]{1,2,0:T(8,128)(2,1)S(1)} %slice_bitcast_fusion, bf16[1,1024,1536]{1,2,0:T(8,128)(2,1)} %collective-permute-done), kind=kLoop, calls=%fused_computation.8 | loop fusion | flops 9437184 | bytes 18874368 | tf_op jit(solution)/shard_map/concatenate | solution.py:22
  283.1 7.2 %fusion.406 = (bf16[3,1024,768]{1,2,0:T(8,128)(2,1)}, bf16[3,1024,768]{1,2,0:T(8,128)(2,1)S(1)}) fusion(bf16[3,1024,1536]{1,2,0:T(8,128)(2,1)} %pad_maximum_fusion), kind=kLoop, calls=%fused_computation.634 | loop fusion | bytes 18874368 | tf_op jit(solution)/shard_map/slice | solution.py:113
  325.7 5.0 fusion.43
  330.7 5.3 fusion.44
  336.1 4.7 fusion.45
  340.9 10.0 %fusion.109 = (f32[512]{0:T(512)S(1)}, f32[512]{0:T(512)S(1)}, f32[512]{0:T(512)S(1)}, f32[512]{0:T(512)S(1)}, f32[512]{0:T(512)S(1)}, /*index=5*/f32[512]{0:T(512)S(1)}) fusion(pred[512,1024]{1,0:T(32,128)(4,1)} %copy.164, f32[512,1024]{1,0:T(8,128)} %get-tuple-element.202, f32[512]{0:T(512)S(1)} %get-tuple-element.167, f32[512]{0:T(512)S(1)} %get-tuple-element.166, ...), kind=kLoop, calls=%fused_computation.192 | loop fusion | flops 15725568 | bytes 13131776 | tf_op jit(solution)/shard_map/reduce_sum | solution.py:141
  350.8 6.6 %fusion.111 = (f32[512]{0:T(512)S(1)}, f32[512]{0:T(512)S(1)}, f32[512]{0:T(512)S(1)}, f32[512]{0:T(512)S(1)}, f32[512]{0:T(512)S(1)}, /*index=5*/f32[512]{0:T(512)S(1)}) fusion(pred[512,1024]{1,0:T(32,128)(4,1)S(1)} %copy-done.28, f32[512,1024]{1,0:T(8,128)} %get-tuple-element.201, f32[512]{0:T(512)S(1)} %get-tuple-element.121, ...), kind=kLoop, calls=%fused_computation.194 | loop fusion | flops 15725568 | bytes 13131776 | tf_op jit(solution)/shard_map/reduce_sum | solution.py:141
  357.4 6.6 %fusion.113 = (f32[512]{0:T(512)S(1)}, f32[512]{0:T(512)S(1)}, f32[512]{0:T(512)S(1)}, f32[512]{0:T(512)S(1)}, f32[512]{0:T(512)S(1)}, /*index=5*/f32[512]{0:T(512)S(1)}) fusion(pred[512,1024]{1,0:T(32,128)(4,1)S(1)} %copy-done.29, f32[512,1024]{1,0:T(8,128)} %get-tuple-element.200, f32[512]{0:T(512)S(1)} %get-tuple-element.120, ...), kind=kLoop, calls=%fused_computation.196 | loop fusion | flops 15725568 | bytes 13131776 | tf_op jit(solution)/shard_map/reduce_sum | solution.py:141
  370.6 5.3 fusion.46
  376.0 4.7 fusion.47
  380.7 4.7 fusion.48
  385.4 10.2 %fusion.115 = (f32[512]{0:T(512)S(1)}, f32[512]{0:T(512)S(1)}, f32[512]{0:T(512)S(1)}, f32[512]{0:T(512)S(1)}, f32[512]{0:T(512)S(1)}, /*index=5*/f32[512]{0:T(512)S(1)}) fusion(pred[512,1024]{1,0:T(32,128)(4,1)} %copy.170, f32[512,1024]{1,0:T(8,128)} %get-tuple-element.199, f32[512]{0:T(512)S(1)} %get-tuple-element.180, f32[512]{0:T(512)S(1)} %get-tuple-element.179, ...), kind=kLoop, calls=%fused_computation.198 | loop fusion | flops 15725568 | bytes 13131776 | tf_op jit(solution)/shard_map/reduce_sum | solution.py:141
  395.7 9.3 %fusion.117 = (f32[512]{0:T(512)S(1)}, f32[512]{0:T(512)S(1)}, f32[512]{0:T(512)S(1)}, f32[512]{0:T(512)S(1)}, f32[512]{0:T(512)S(1)}, /*index=5*/f32[512]{0:T(512)S(1)}) fusion(pred[512,1024]{1,0:T(32,128)(4,1)} %copy.172, f32[512,1024]{1,0:T(8,128)} %get-tuple-element.198, f32[512]{0:T(512)S(1)} %get-tuple-element.136, f32[512]{0:T(512)S(1)} %get-tuple-element.134, ...), kind=kLoop, calls=%fused_computation.200 | loop fusion | flops 15725568 | bytes 13131776 | tf_op jit(solution)/shard_map/reduce_sum | solution.py:141
  405.0 9.3 %fusion.119 = (f32[512]{0:T(512)S(1)}, f32[512]{0:T(512)S(1)}, f32[512]{0:T(512)S(1)}, f32[512]{0:T(512)S(1)}, f32[512]{0:T(512)S(1)}, /*index=5*/f32[512]{0:T(512)S(1)}) fusion(pred[512,1024]{1,0:T(32,128)(4,1)} %copy.174, f32[512,1024]{1,0:T(8,128)} %get-tuple-element.197, f32[512]{0:T(512)S(1)} %get-tuple-element.135, f32[512]{0:T(512)S(1)} %get-tuple-element.133, ...), kind=kLoop, calls=%fused_computation.202 | loop fusion | flops 15725568 | bytes 13131776 | tf_op jit(solution)/shard_map/reduce_sum | solution.py:141
  459.0 9.4 %convolution_convert_fusion = bf16[1024,3072]{1,0:T(8,128)(2,1)} fusion(bf16[1024,768]{0,1:T(8,128)(2,1)S(1)} %bitcast.461, bf16[768,3072]{1,0:T(8,128)(2,1)} %all-gather.9.cloned.1.call-done), kind=kOutput, calls=%fused_computation.15 | convolution fusion | flops 4834983936 | bytes 12582912 | tf_op jit(solution)/shard_map/dot_general | solution.py:154
  468.4 146.0 %reduce-scatter.2.cloned.1.call-done = bf16[256,3072]{1,0:T(8,128)(2,1)} async-done(((bf16[1024,3072]{1,0:T(8,128)(2,1)}), bf16[256,3072]{1,0:T(8,128)(2,1)}) %reduce-scatter.2.cloned.1.call-update) | async-done | bytes 1572880 | tf_op jit(solution)/shard_map/reduce_scatter | solution.py:153
  (254 shorter events, 113.7 us)
Async XLA Ops:
  6.5 7.6 %copy-start = (bf16[256,3,192]{0,2,1:T(8,128)(2,1)S(1)}, bf16[256,3,192]{0,2,1:T(8,128)(2,1)}, u32[]{:S(2)}) copy-start(bf16[256,3,192]{0,2,1:T(8,128)(2,1)} %param.12) | copy-start | bytes 884740
  6.5 121.4 %all-gather.5.cloned.1.call-start = ((), (), s32[]{:S(2)}) async-start(), calls=%async_computation.1 | async-start | bytes 7864320 | tf_op jit(solution)/shard_map/all_gather | solution.py:103
  7.3 211.7 %all-gather.7.cloned.1.call-start = ((), (), s32[]{:S(2)}) async-start(), calls=%async_computation.2 | async-start | bytes 17694720 | tf_op jit(solution)/shard_map/all_gather | solution.py:96
  13.4 445.6 %all-gather.9.cloned.1.call-start = ((), (), s32[]{:S(2)}) async-start(), calls=%async_computation.3 | async-start | bytes 5898240 | tf_op jit(solution)/shard_map/all_gather | solution.py:97
  127.9 4.6 copy-start.2
  242.3 20.3 %copy-start.39 = (s32[4,16]{1,0:T(4,128)S(1)}, s32[4,16]{1,0:T(4,128)}, u32[]{:S(2)}) copy-start(s32[4,16]{1,0:T(4,128)} %param.15) | copy-start | bytes 772
  244.4 31.0 %collective-permute-start = (bf16[1,1024,1536]{1,2,0:T(8,128)(2,1)S(1)}, bf16[1,1024,1536]{1,2,0:T(8,128)(2,1)}, u32[]{:S(2)}, u32[]{:S(2)}) collective-permute-start(bf16[1,1024,1536]{1,2,0:T(8,128)(2,1)S(1)} %slice_bitcast_fusion), channel_id=1, source_target_pairs={{0,4},{4,8},{8,12},{1,5},{5,9},{9,13},{2,6},{6,10},{10,14},{3,7},{... | collective-permute-start | bytes 9437192 | tf_op jit(solution)/shard_map/ppermute | solution.py:18
  248.3 27.1 %collective-permute-start.1 = (bf16[1,1024,1536]{1,2,0:T(8,128)(2,1)S(1)}, bf16[1,1024,1536]{1,2,0:T(8,128)(2,1)}, u32[]{:S(2)}, u32[]{:S(2)}) collective-permute-start(bf16[1,1024,1536]{1,2,0:T(8,128)(2,1)S(1)} %slice_bitcast_fusion), channel_id=1, source_target_pairs={{4,0},{8,4},{12,8},{5,1},{9,5},{13,9},{6,2},{10,6},{14,10},{7,3},{... | collective-permute-start | bytes 9437192 | tf_op jit(solution)/shard_map/ppermute | solution.py:21
  249.6 364.8 %reduce-scatter.2.cloned.1.call-start = ((), (), s32[]{:S(2)}) async-start(), calls=%async_computation.4 | async-start | bytes 7864320 | tf_op jit(solution)/shard_map/reduce_scatter | solution.py:153
  303.3 32.8 %copy-start.7 = (f32[512,1024]{1,0:T(8,128)}, f32[512,1024]{1,0:T(8,128)S(1)}, u32[]{:S(2)}) copy-start(f32[512,1024]{1,0:T(8,128)S(1)} %fusion.221) | copy-start | bytes 6291460
  325.7 5.0 copy-start.28
  330.7 5.4 copy-start.29
  370.6 5.3 copy-start.4
  370.6 5.3 copy-start.34
  375.9 4.7 copy-start.32
  385.4 10.2 %copy-start.5 = (f32[512,1024]{1,0:T(8,128)S(1)}, f32[512,1024]{1,0:T(8,128)}, u32[]{:S(2)}) copy-start(f32[512,1024]{1,0:T(8,128)} %fusion.218) | copy-start | bytes 6291460
  385.4 10.2 %copy-start.13 = (f32[512,1024]{1,0:T(8,128)S(1)}, f32[512,1024]{1,0:T(8,128)}, u32[]{:S(2)}) copy-start(f32[512,1024]{1,0:T(8,128)} %fusion.224) | copy-start | bytes 6291460
  395.7 9.3 %copy-start.12 = (f32[512,1024]{1,0:T(8,128)S(1)}, f32[512,1024]{1,0:T(8,128)}, u32[]{:S(2)}) copy-start(f32[512,1024]{1,0:T(8,128)} %fusion.226) | copy-start | bytes 6291460
  414.3 2.9 copy-start.18
  424.8 5.4 slice-start
  426.7 3.5 slice-start.1
  468.4 146.0 %copy-start.27 = (bf16[256,3072]{1,0:T(8,128)(2,1)S(1)}, bf16[256,3072]{1,0:T(8,128)(2,1)}, u32[]{:S(2)}) copy-start(bf16[256,3072]{1,0:T(8,128)(2,1)} %param.9) | copy-start | bytes 4718596
  468.4 146.0 %copy-start.38 = (f32[1,3072]{1,0:T(1,128)S(1)}, f32[1,3072]{1,0:T(1,128)}, u32[]{:S(2)}) copy-start(f32[1,3072]{1,0:T(1,128)} %get-tuple-element.149) | copy-start | bytes 36868
  614.4 3.2 copy-start.1
  (26 other events, 44.8 us)
Sparse Core Ops, SparseCore 0:
  8.9 118.9 all-gather.4
  129.5 89.4 all-gather.6
  249.7 50.9 all-gather.8
  468.5 145.8 reduce-scatter.1
where the time goes:
time: 633 us; the launch traced here: 624 us
  waiting for transfers between devices  307 us (48%)
  matrix products  136 us (21%)
  other arithmetic  72.7 us (11%)
  local copies, waits for them, and re-layouts  39.1 us (6%)
  blocking collectives  37.1 us (6%)
  starting transfers between devices  17.5 us (3%)
  between operations  15.1 us (2%)
    reduce_scatter x1, waiting for transfers between devices, body(): lax.psum_scatter(jnp.dot(attended, out_full, preferred_element_type=jnp.f...  146 us
    all_gather x1, waiting for transfers between devices, body(): qkv_full = lax.all_gather(qkv_weight, 'seq', axis=0, tiled=True)  84.6 us
    all_gather x1, waiting for transfers between devices, body(): lax.all_gather(latents, 'fsdp', axis=0, tiled=True)  75.7 us
    dot_general x36, matrix products, body(): lax.dot_general(queries, key_all[key_blk, :, head_idx], (((1,), (1,)), ((...  65 us
    reduce_sum x6, other arithmetic, body(): running_total = running_total * factor + jnp.sum(weights, axis=1)  52 us
    dot_general x36, matrix products, body(): jnp.dot(weights.astype(jnp.bfloat16), value_all[key_blk, :, head_idx], pr...  41 us
    all_gather x1, blocking collectives, body(): modulation = lax.all_gather(own_mod, ('seq', 'fsdp'), axis=1, tiled=True)  37.1 us
    dot_general x1, matrix products, project_rows(): mixture = jnp.dot(normed, weight_flat, preferred_element_type=jnp.float32)  20 us
  transfers between devices with their start and end apart: 6, of which 3 were waited for; matrix products, arithmetic and copies ran while one was open for 32% of the time, Pallas kernels for 0%

commit v1 on v0

--- a/solution.py
+++ b/solution.py
@@ -93,7 +93,13 @@
     shift_mod = modulation[0]
     scale_mod = modulation[1]
     gate_mod = modulation[2]
-    qkv_full = lax.all_gather(qkv_weight, "seq", axis=0, tiled=True)
+    size = lax.axis_size("seq")
+    held, parts = (qkv_weight, [qkv_weight])
+    for _ in range(size - 1):
+        held = lax.ppermute(held, "seq", [(i_2, (i_2 + 1) % size) for i_2 in range(size)])
+        parts.insert(0, held)
+    row_of_blocks = jnp.concatenate(parts, axis=0)
+    qkv_full = jnp.roll(row_of_blocks, (lax.axis_index("seq") + 1) * qkv_weight.shape[0], axis=0)
     out_full = lax.all_gather(out_weight, "seq", axis=1, tiled=True)
     model_width = qkv_full.shape[0]
     group_width = qkv_full.shape[2]

time: 633 us -> 605 us (0.956)
  waiting for transfers between devices: 307 us -> 241 us
  local copies, waits for them, and re-layouts: 39.1 us -> 79.4 us
  starting transfers between devices: 17.5 us -> 5.71 us
  other arithmetic: 72.7 us -> 79.5 us
    all_gather x1 -> x0, waiting for transfers between devices: 84.6 us -> none  [body(): qkv_full = lax.all_gather(qkv_weight, 'seq', axis=0, tiled=True)]
    ppermute x0 -> x3, waiting for transfers between devices: none -> 82.3 us  [body(): lax.ppermute(held, 'seq', [(i_2, (i_2 + 1) % size) for i_2 in range(size)])]
    all_gather x1, waiting for transfers between devices: 75.7 us -> 0.01 us  [body(): lax.all_gather(latents, 'fsdp', axis=0, tiled=True)]
    unnamed x91 -> x124, local copies, waits for them, and re-layouts: 17.7 us -> 40.2 us
    dynamic_slice x0 -> x1, local copies, waits for them, and re-layouts: none -> 15.8 us  [body(): jnp.roll(row_of_blocks, (lax.axis_index('seq') + 1) * qkv_weight.shape[0]...]
    reduce_scatter x1, starting transfers between devices: 12.3 us -> 0.21 us  [body(): lax.psum_scatter(jnp.dot(attended, out_full, preferred_element_type=jnp.f...]
    reduce_scatter x1, waiting for transfers between devices: 146 us -> 158 us  [body(): lax.psum_scatter(jnp.dot(attended, out_full, preferred_element_type=jnp.f...]
    dot_general x36, matrix products: 41 us -> 47.5 us  [body(): jnp.dot(weights.astype(jnp.bfloat16), value_all[key_blk, :, head_idx], pr...]
  transfers between devices with their start and end apart: 6 -> 8, of which waited for: 3 -> 3; matrix products, arithmetic and copies ran while one was open for 32% -> 36% of each run, Pallas kernels for 0% -> 0%
where the time goes in v1:
time: 605 us; the launch traced here: 599 us
  waiting for transfers between devices  241 us (40%)
  matrix products  141 us (23%)
  other arithmetic  79.5 us (13%)
  local copies, waits for them, and re-layouts  79.4 us (13%)
  blocking collectives  36.2 us (6%)
  between operations  17 us (3%)
    reduce_scatter x1, waiting for transfers between devices, body(): lax.psum_scatter(jnp.dot(attended, out_full, preferred_element_type=jnp.f...  158 us
    ppermute x3, waiting for transfers between devices, body(): lax.ppermute(held, 'seq', [(i_2, (i_2 + 1) % size) for i_2 in range(size)])  82.3 us
    dot_general x36, matrix products, body(): lax.dot_general(queries, key_all[key_blk, :, head_idx], (((1,), (1,)), ((...  64.9 us
    reduce_sum x6, other arithmetic, body(): running_total = running_total * factor + jnp.sum(weights, axis=1)  53.4 us
    dot_general x36, matrix products, body(): jnp.dot(weights.astype(jnp.bfloat16), value_all[key_blk, :, head_idx], pr...  47.5 us
    unnamed x124, local copies, waits for them, and re-layouts  40.2 us
    all_gather x1, blocking collectives, body(): modulation = lax.all_gather(own_mod, ('seq', 'fsdp'), axis=1, tiled=True)  36.2 us
    dot_general x1, matrix products, project_rows(): mixture = jnp.dot(normed, weight_flat, preferred_element_type=jnp.float32)  18.8 us
  transfers between devices with their start and end apart: 8, of which 3 were waited for; matrix products, arithmetic and copies ran while one was open for 36% of the time, Pallas kernels for 0%

profile of v1, /device:TPU:0, one launch (start us, length us, event | category | flops | bytes accessed | tf_op | source)
XLA Modules:
  0.0 599.3 jit_solution(7494153632940384450)
XLA Ops:
  8.1 6.0 %copy.167 = bf16[768,3,768]{0,2,1:T(8,128)(2,1)} copy(bf16[768,3,768]{2,0,1:T(8,128)(2,1)} %param.10) | data formatting | bytes 7077888 | tf_op args[1]
  14.6 41.3 %collective-permute-done = bf16[768,3,768]{0,2,1:T(8,128)(2,1)S(1)} collective-permute-done((bf16[768,3,768]{0,2,1:T(8,128)(2,1)}, bf16[768,3,768]{0,2,1:T(8,128)(2,1)S(1)}, u32[]{:S(2)}, u32[]{:S(2)}) %collective-permute-start) | collective-permute-done | bytes 3538976 | tf_op jit(solution)/shard_map/ppermute | solution.py:99
  57.8 41.0 %collective-permute-done.1 = bf16[768,3,768]{0,2,1:T(8,128)(2,1)} collective-permute-done((bf16[768,3,768]{0,2,1:T(8,128)(2,1)S(1)}, bf16[768,3,768]{0,2,1:T(8,128)(2,1)}, u32[]{:S(2)}, u32[]{:S(2)}) %collective-permute-start.1) | collective-permute-done | bytes 3538976 | tf_op jit(solution)/shard_map/ppermute | solution.py:99
  99.7 36.2 %all-gather = f32[16,192,3]{1,2,0:T(4,128)S(1)} all-gather(f32[1,192,3]{1,2,0:T(4,128)S(1)} %bitcast.465), channel_id=1, replica_groups=mesh['group'=2,'seq'=4,'fsdp'=4] {'seq','fsdp'}, dimensions={0}, use_global_device_ids=true | all-gather | bytes 39168 | tf_op jit(solution)/shard_map/all_gather | solution.py:92
  147.1 4.2 constant_dynamic-update-slice_fusion.6
  160.8 4.2 constant_dynamic-update-slice_fusion.2
  169.2 15.8 %constant_dynamic-slice_fusion.1 = bf16[3072,3,768]{0,2,1:T(8,128)(2,1)} fusion(bf16[6144,3,768]{0,2,1:T(8,128)(2,1)} %constant_dynamic-update-slice_fusion, s32[]{:T(128)S(6)} %select_n.279), kind=kLoop, calls=%fused_computation.467 | loop fusion | bytes 28311556 | tf_op jit(solution)/shard_map/jit(_roll_dynamic)/dynamic_slice | solution.py:102
  185.0 18.8 %fusion.7 = f32[1024,3,6,128]{0,3,2,1:T(8,128)S(1)} fusion(bf16[3,6,128,3072]{3,2,1,0:T(8,128)(2,1)} %bitcast.417, bf16[1024,3072]{1,0:T(8,128)(2,1)S(1)} %copy-done.3, f32[3072]{0:T(1024)S(1)} %bitcast.466, f32[3072]{0:T(1024)S(1)} %bitcast.467, f32[1024]{0:T(1024)S(1)} %add_rsqrt_fusion.2, f32[1024]{0:T(1024)S(1)} %broadcast_multiply_fusion), kind=kOutput, calls=%fused_computation.10 | convolution fusion | flops 14514388992 | bytes 29917184 | tf_op jit(solution)/shard_map/dot_general | solution.py:46
  227.9 8.0 %pad_maximum_fusion = bf16[3,1024,1536]{1,2,0:T(8,128)(2,1)} fusion(bf16[1,1024,1536]{1,2,0:T(8,128)(2,1)} %collective-permute-done.4, bf16[1,1024,1536]{1,2,0:T(8,128)(2,1)S(1)} %slice_bitcast_fusion, bf16[1,1024,1536]{1,2,0:T(8,128)(2,1)} %collective-permute-done.3), kind=kLoop, calls=%fused_computation.8 | loop fusion | flops 9437184 | bytes 18874368 | tf_op jit(solution)/shard_map/concatenate | solution.py:22
  235.8 7.1 %fusion.406 = (bf16[3,1024,768]{1,2,0:T(8,128)(2,1)}, bf16[3,1024,768]{1,2,0:T(8,128)(2,1)S(1)}) fusion(bf16[3,1024,1536]{1,2,0:T(8,128)(2,1)} %pad_maximum_fusion), kind=kLoop, calls=%fused_computation.643 | loop fusion | bytes 18874368 | tf_op jit(solution)/shard_map/slice | solution.py:119
  278.2 5.0 fusion.43
  283.2 5.4 fusion.44
  288.6 4.7 fusion.45
  295.6 10.1 %fusion.109 = (f32[512]{0:T(512)S(1)}, f32[512]{0:T(512)S(1)}, f32[512]{0:T(512)S(1)}, f32[512]{0:T(512)S(1)}, f32[512]{0:T(512)S(1)}, /*index=5*/f32[512]{0:T(512)S(1)}) fusion(pred[512,1024]{1,0:T(32,128)(4,1)} %copy.170, f32[512,1024]{1,0:T(8,128)} %get-tuple-element.202, f32[512]{0:T(512)S(1)} %get-tuple-element.167, f32[512]{0:T(512)S(1)} %get-tuple-element.166, ...), kind=kLoop, calls=%fused_computation.192 | loop fusion | flops 15725568 | bytes 13131776 | tf_op jit(solution)/shard_map/reduce_sum | solution.py:147
  305.7 6.6 %fusion.111 = (f32[512]{0:T(512)S(1)}, f32[512]{0:T(512)S(1)}, f32[512]{0:T(512)S(1)}, f32[512]{0:T(512)S(1)}, f32[512]{0:T(512)S(1)}, /*index=5*/f32[512]{0:T(512)S(1)}) fusion(pred[512,1024]{1,0:T(32,128)(4,1)S(1)} %copy-done.32, f32[512,1024]{1,0:T(8,128)} %get-tuple-element.201, f32[512]{0:T(512)S(1)} %get-tuple-element.121, ...), kind=kLoop, calls=%fused_computation.194 | loop fusion | flops 15725568 | bytes 13131776 | tf_op jit(solution)/shard_map/reduce_sum | solution.py:147
  312.3 6.6 %fusion.113 = (f32[512]{0:T(512)S(1)}, f32[512]{0:T(512)S(1)}, f32[512]{0:T(512)S(1)}, f32[512]{0:T(512)S(1)}, f32[512]{0:T(512)S(1)}, /*index=5*/f32[512]{0:T(512)S(1)}) fusion(pred[512,1024]{1,0:T(32,128)(4,1)S(1)} %copy-done.33, f32[512,1024]{1,0:T(8,128)} %get-tuple-element.200, f32[512]{0:T(512)S(1)} %get-tuple-element.120, ...), kind=kLoop, calls=%fused_computation.196 | loop fusion | flops 15725568 | bytes 13131776 | tf_op jit(solution)/shard_map/reduce_sum | solution.py:147
  325.5 5.3 fusion.46
  330.8 4.7 fusion.47
  335.6 4.7 fusion.48
  343.2 10.2 %fusion.115 = (f32[512]{0:T(512)S(1)}, f32[512]{0:T(512)S(1)}, f32[512]{0:T(512)S(1)}, f32[512]{0:T(512)S(1)}, f32[512]{0:T(512)S(1)}, /*index=5*/f32[512]{0:T(512)S(1)}) fusion(pred[512,1024]{1,0:T(32,128)(4,1)} %copy.176, f32[512,1024]{1,0:T(8,128)} %get-tuple-element.199, f32[512]{0:T(512)S(1)} %get-tuple-element.180, f32[512]{0:T(512)S(1)} %get-tuple-element.179, ...), kind=kLoop, calls=%fused_computation.198 | loop fusion | flops 15725568 | bytes 13131776 | tf_op jit(solution)/shard_map/reduce_sum | solution.py:147
  353.5 9.8 %fusion.117 = (f32[512]{0:T(512)S(1)}, f32[512]{0:T(512)S(1)}, f32[512]{0:T(512)S(1)}, f32[512]{0:T(512)S(1)}, f32[512]{0:T(512)S(1)}, /*index=5*/f32[512]{0:T(512)S(1)}) fusion(pred[512,1024]{1,0:T(32,128)(4,1)} %copy.178, f32[512,1024]{1,0:T(8,128)} %get-tuple-element.198, f32[512]{0:T(512)S(1)} %get-tuple-element.136, f32[512]{0:T(512)S(1)} %get-tuple-element.134, ...), kind=kLoop, calls=%fused_computation.200 | loop fusion | flops 15725568 | bytes 13131776 | tf_op jit(solution)/shard_map/reduce_sum | solution.py:147
  363.3 10.1 %fusion.119 = (f32[512]{0:T(512)S(1)}, f32[512]{0:T(512)S(1)}, f32[512]{0:T(512)S(1)}, f32[512]{0:T(512)S(1)}, f32[512]{0:T(512)S(1)}, /*index=5*/f32[512]{0:T(512)S(1)}) fusion(pred[512,1024]{1,0:T(32,128)(4,1)} %copy.180, f32[512,1024]{1,0:T(8,128)} %get-tuple-element.197, f32[512]{0:T(512)S(1)} %get-tuple-element.135, f32[512]{0:T(512)S(1)} %get-tuple-element.133, ...), kind=kLoop, calls=%fused_computation.202 | loop fusion | flops 15725568 | bytes 13131776 | tf_op jit(solution)/shard_map/reduce_sum | solution.py:147
  421.4 9.4 %convolution_convert_fusion = bf16[1024,3072]{1,0:T(8,128)(2,1)} fusion(bf16[1024,768]{0,1:T(8,128)(2,1)S(1)} %bitcast.462, bf16[768,3072]{1,0:T(8,128)(2,1)} %all-gather.6.cloned.1.call-done), kind=kOutput, calls=%fused_computation.15 | convolution fusion | flops 4834983936 | bytes 12582912 | tf_op jit(solution)/shard_map/dot_general | solution.py:160
  430.8 157.7 %reduce-scatter.2.cloned.1.call-done = bf16[256,3072]{1,0:T(8,128)(2,1)} async-done(((bf16[1024,3072]{1,0:T(8,128)(2,1)}), bf16[256,3072]{1,0:T(8,128)(2,1)}) %reduce-scatter.2.cloned.1.call-update) | async-done | bytes 1572880 | tf_op jit(solution)/shard_map/reduce_scatter | solution.py:159
  (292 shorter events, 149.5 us)
Async XLA Ops:
  7.4 92.2 %copy-start = (bf16[256,3,192]{0,2,1:T(8,128)(2,1)S(1)}, bf16[256,3,192]{0,2,1:T(8,128)(2,1)}, u32[]{:S(2)}) copy-start(bf16[256,3,192]{0,2,1:T(8,128)(2,1)} %param.12) | copy-start | bytes 884740
  7.4 129.3 %all-gather.4.cloned.1.call-start = ((), (), s32[]{:S(2)}) async-start(), calls=%async_computation.1 | async-start | bytes 7864320 | tf_op jit(solution)/shard_map/all_gather | solution.py:109
  8.1 413.3 %all-gather.6.cloned.1.call-start = ((), (), s32[]{:S(2)}) async-start(), calls=%async_computation.2 | async-start | bytes 5898240 | tf_op jit(solution)/shard_map/all_gather | solution.py:103
  14.2 41.8 %collective-permute-start = (bf16[768,3,768]{0,2,1:T(8,128)(2,1)}, bf16[768,3,768]{0,2,1:T(8,128)(2,1)S(1)}, u32[]{:S(2)}, u32[]{:S(2)}) collective-permute-start(bf16[768,3,768]{0,2,1:T(8,128)(2,1)} %copy.167), channel_id=1, source_target_pairs={{0,4},{4,8},{8,12},{12,0},{1,5},{5,9},{9,13},{13,1},{2,6},{6,10},{... | collective-permute-start | bytes 10616840 | tf_op jit(solution)/shard_map/ppermute | solution.py:99
  57.8 41.0 %collective-permute-start.1 = (bf16[768,3,768]{0,2,1:T(8,128)(2,1)S(1)}, bf16[768,3,768]{0,2,1:T(8,128)(2,1)}, u32[]{:S(2)}, u32[]{:S(2)}) collective-permute-start(bf16[768,3,768]{0,2,1:T(8,128)(2,1)S(1)} %collective-permute-done), channel_id=1, source_target_pairs={{0,4},{4,8},{8,12},{12,0},{1,5},{5,9},{9,13},{13,1},{2,6},{6,10},{... | collective-permute-start | bytes 10616840 | tf_op jit(solution)/shard_map/ppermute | solution.py:99
  98.8 44.3 %collective-permute-start.2 = (bf16[768,3,768]{0,2,1:T(8,128)(2,1)}, bf16[768,3,768]{0,2,1:T(8,128)(2,1)}, u32[]{:S(2)}, u32[]{:S(2)}) collective-permute-start(bf16[768,3,768]{0,2,1:T(8,128)(2,1)} %collective-permute-done.1), channel_id=1, source_target_pairs={{0,4},{4,8},{8,12},{12,0},{1,5},{5,9},{9,13},{13,1},{2,6},{6,10},{... | collective-permute-start | bytes 10616840 | tf_op jit(solution)/shard_map/ppermute | solution.py:99
  136.7 4.6 copy-start.3
  147.1 4.2 copy-start.24
  207.0 8.0 %copy-start.52 = (s32[4,16]{1,0:T(4,128)S(1)}, s32[4,16]{1,0:T(4,128)}, u32[]{:S(2)}) copy-start(s32[4,16]{1,0:T(4,128)} %param.15) | copy-start | bytes 772
  209.2 18.7 %collective-permute-start.3 = (bf16[1,1024,1536]{1,2,0:T(8,128)(2,1)S(1)}, bf16[1,1024,1536]{1,2,0:T(8,128)(2,1)}, u32[]{:S(2)}, u32[]{:S(2)}) collective-permute-start(bf16[1,1024,1536]{1,2,0:T(8,128)(2,1)S(1)} %slice_bitcast_fusion), channel_id=1, source_target_pairs={{0,4},{4,8},{8,12},{1,5},{5,9},{9,13},{2,6},{6,10},{10,14},{3,7},{... | collective-permute-start | bytes 9437192 | tf_op jit(solution)/shard_map/ppermute | solution.py:18
  212.8 15.0 %collective-permute-start.4 = (bf16[1,1024,1536]{1,2,0:T(8,128)(2,1)S(1)}, bf16[1,1024,1536]{1,2,0:T(8,128)(2,1)}, u32[]{:S(2)}, u32[]{:S(2)}) collective-permute-start(bf16[1,1024,1536]{1,2,0:T(8,128)(2,1)S(1)} %slice_bitcast_fusion), channel_id=1, source_target_pairs={{4,0},{8,4},{12,8},{5,1},{9,5},{13,9},{6,2},{10,6},{14,10},{7,3},{... | collective-permute-start | bytes 9437192 | tf_op jit(solution)/shard_map/ppermute | solution.py:21
  214.1 374.4 %reduce-scatter.2.cloned.1.call-start = ((), (), s32[]{:S(2)}) async-start(), calls=%async_computation.3 | async-start | bytes 7864320 | tf_op jit(solution)/shard_map/reduce_scatter | solution.py:159
  255.9 32.7 %copy-start.8 = (f32[512,1024]{1,0:T(8,128)}, f32[512,1024]{1,0:T(8,128)S(1)}, u32[]{:S(2)}) copy-start(f32[512,1024]{1,0:T(8,128)S(1)} %fusion.221) | copy-start | bytes 6291460
  278.2 5.0 copy-start.32
  283.2 5.4 copy-start.33
  325.5 5.3 copy-start.5
  325.5 5.3 copy-start.38
  330.8 4.8 copy-start.36
  343.2 10.2 %copy-start.6 = (f32[512,1024]{1,0:T(8,128)S(1)}, f32[512,1024]{1,0:T(8,128)}, u32[]{:S(2)}) copy-start(f32[512,1024]{1,0:T(8,128)} %fusion.218) | copy-start | bytes 6291460
  343.2 10.2 %copy-start.15 = (f32[512,1024]{1,0:T(8,128)S(1)}, f32[512,1024]{1,0:T(8,128)}, u32[]{:S(2)}) copy-start(f32[512,1024]{1,0:T(8,128)} %fusion.224) | copy-start | bytes 6291460
  353.4 9.8 %copy-start.13 = (f32[512,1024]{1,0:T(8,128)S(1)}, f32[512,1024]{1,0:T(8,128)}, u32[]{:S(2)}) copy-start(f32[512,1024]{1,0:T(8,128)} %fusion.226) | copy-start | bytes 6291460
  395.0 5.4 slice-start
  430.8 157.7 %copy-start.31 = (bf16[256,3072]{1,0:T(8,128)(2,1)S(1)}, bf16[256,3072]{1,0:T(8,128)(2,1)}, u32[]{:S(2)}) copy-start(bf16[256,3072]{1,0:T(8,128)(2,1)} %param.9) | copy-start | bytes 4718596
  430.8 157.7 %copy-start.42 = (f32[1,3072]{1,0:T(1,128)S(1)}, f32[1,3072]{1,0:T(1,128)}, u32[]{:S(2)}) copy-start(f32[1,3072]{1,0:T(1,128)} %get-tuple-element.149) | copy-start | bytes 36868
  (41 other events, 77.3 us)
Sparse Core Ops, SparseCore 0:
  9.8 119.0 all-gather.3
  431.0 157.4 reduce-scatter.1
Sparse Core Ops, SparseCore 1:
  214.2 49.9 all-gather.5
